TPU v7x, 32 devices: a whole 2x2x4 slice. The times are simulated.
32 devices in a mesh: section: 2 (over core), row: 4 (over y, x), col: 4 (over z).
Axes of the slice: x: 2, y: 2, z: 4, core: 2. Of those that a mesh axis runs over, the one named last changes fastest.
Arguments:
- out_grad: bfloat16 [2048, 256], P(('row', 'col')), may hold values from -6 to 6
- pre_act: bfloat16 [2, 2048, 256], P('section', ('row', 'col')), may hold values from -6 to 6
- aggregated: bfloat16 [2, 2048, 256], P('section', ('row', 'col')), may hold values from -6 to 6
- weights: bfloat16 [2, 256, 256], P('section'), may hold values from -0.375 to 0.375
- tiles: bfloat16 [4, 4, 64, 128, 128], P('row', 'col'), may hold values from -0.109375 to 0.109375
- tile_index: int32 [4, 4, 64, 2], P('row', 'col'), may hold values from 0 to 3, as said below
- live_count: int32 [4, 4], P('row', 'col'), may hold values from 8 to 64, as said below
Outputs:
- weight_grad: float32 [2, 256, 256], P('section')
- feature_grads: bfloat16 [2, 2048, 256], P('section', ('row', 'col'))
Inputs may be any that keep to these rules, and one draw needn't show every extreme that they name: `tile_index`: both entries index blocks of the tile: the first is under 4, the second under 4. `live_count`: some tile uses all 64 slots.
All inputs are finite; a program needn't handle non-finite values.
Results may differ from a plain program's by a relative error of at most 0.012.
Values may be sent and summed in bfloat16 or wider, within the bound.
A program may use at most 64 MiB of HBM per device.

v0:
```python
import math
import jax
import jax.numpy as jnp
from jax import lax
from jax.sharding import PartitionSpec as P


def from_behind(value, axis, steps):
    count = lax.axis_size(axis)
    leading, last = (max(0, -steps), min(count, count - steps))
    return lax.ppermute(value, axis, [(source, source + steps) for source in range(leading, last)])


def on_device(out_grad, pre_act, aggregated, weights, tiles, tile_index, live_count):
    section_id = lax.axis_index("section")
    upper = section_id == 1
    pre_layer = pre_act[0]
    saved_agg = aggregated[0]
    weight_mat = weights[0]
    tile_blocks = tiles[0, 0]
    tile_slots = tile_index[0, 0]
    tile_count = live_count[0, 0]
    node_rows = out_grad.shape[0]
    width = out_grad.shape[1]
    slot_total = tile_blocks.shape[0]
    block = tile_blocks.shape[1]
    tile_rows = node_rows * lax.axis_size("col")
    row_blocks = tile_rows // block
    group = min(32, slot_total)
    groups = slot_total // group
    grouped_slots = tile_slots.reshape(groups, group, 2)
    all_targets = jnp.arange(row_blocks, dtype=jnp.int32)

    def spread(row_grad):
        return lax.all_gather(row_grad, "row", axis=0, tiled=True)

    def block_total(source, col_blocks):
        height = source.shape[1]
        grouped_blocks = source.reshape(groups, group, height, block)

        def group_term(total, blocks_here, slots_here, first_slot):
            picked = jnp.take(col_blocks, slots_here[:, 1], axis=0)
            products = jnp.einsum(
                "sij,sjf->sif", blocks_here, picked, preferred_element_type=jnp.float32
            )
            slot_ids = first_slot + jnp.arange(group, dtype=jnp.int32)
            live = slot_ids < tile_count
            select = ((slots_here[:, 0][None, :] == all_targets[:, None]) & live[None, :]).astype(
                jnp.float32
            )
            return total + jnp.einsum("bs,sif->bif", select, products)

        start_total = jnp.zeros((row_blocks, height, width), jnp.float32)

        def scan_step(total, group_id):
            blocks_here = lax.dynamic_index_in_dim(grouped_blocks, group_id, 0, False)
            slots_here = lax.dynamic_index_in_dim(grouped_slots, group_id, 0, False)
            return (group_term(total, blocks_here, slots_here, group_id * group), None)

        total, _ = lax.scan(scan_step, start_total, jnp.arange(groups, dtype=jnp.int32))
        return total.reshape(row_blocks * height, width)

    def reduce_col(source, gathered):
        col_blocks = gathered.reshape(-1, block, width)
        height = source.shape[1]
        return lax.psum_scatter(
            block_total(source, col_blocks), "col", scatter_dimension=0, tiled=True
        )

    def local_terms(incoming):
        masked = jnp.where(pre_layer > 0, incoming, jnp.zeros_like(incoming))
        weight_term = lax.dot_general(
            saved_agg, masked, (((0,), (0,)), ((), ())), preferred_element_type=jnp.float32
        )
        row_grad = lax.dot_general(
            masked, weight_mat, (((1,), (1,)), ((), ())), preferred_element_type=jnp.float32
        ).astype(jnp.bfloat16)
        return (weight_term, row_grad)

    def backward_step(incoming):
        weight_term, row_grad = local_terms(incoming)
        summed = reduce_col(tile_blocks, spread(row_grad))
        return (weight_term, summed.astype(jnp.bfloat16))

    first_input = jnp.where(upper, out_grad, jnp.zeros_like(out_grad))
    first_weight, first_grad = backward_step(first_input)
    received = from_behind(first_grad, "section", -1)
    second_weight, second_grad = backward_step(received)
    local_weight = jnp.where(upper, first_weight, second_weight)
    feature_block = jnp.where(upper, first_grad, second_grad)
    total_weight = lax.psum(local_weight, ("row", "col"))
    node_total = node_rows * lax.axis_size("row") * lax.axis_size("col")
    weight_grad = (total_weight * (1.0 / math.sqrt(node_total)))[None]
    return (weight_grad, feature_block[None])


def solution(mesh):
    placed = (
        P(("row", "col"), None),
        P("section", ("row", "col"), None),
        P("section", ("row", "col"), None),
        P("section", None, None),
        P("row", "col", None, None, None),
        P("row", "col", None, None),
        P("row", "col"),
    )
    return jax.shard_map(
        on_device,
        mesh=mesh,
        in_specs=placed,
        out_specs=(P("section", None, None), P("section", ("row", "col"), None)),
        check_vma=False,
    )
```

profile of v0, /device:TPU:0, one launch (start us, length us, event | category | flops | bytes accessed | tf_op | source)
XLA Modules:
  0.0 212.3 jit_solution(15838875846190478118)
XLA Ops:
  7.2 0.0 copy-start
  7.2 0.0 reduce-scatter.3.cloned.1.call-start
  7.2 0.9 broadcast_compare_fusion
  8.1 0.0 copy-done
  8.1 0.2 convolution_convert_fusion.1
  8.3 10.5 %all_gather.6 = bf16[512,256]{1,0:T(8,128)(2,1)S(1)} all-gather(bf16[128,256]{1,0:T(8,128)(2,1)S(1)} %convolution_convert_fusion.1), channel_id=1, replica_groups=mesh['section'=2,'row'=4,'col'=4] {'row'}, dimensions={0}, use_global_device_ids=true | all-gather | bytes 327680 | tf_op jit(solution)/shard_map/all_gather | solution.py:35
  18.8 0.8 reshape_squeeze.7
  19.6 0.0 copy-start.2
  19.6 0.0 copy-start.3
  19.6 20.1 %while.22 = (s32[]{:T(128)}, f32[4,128,256]{2,0,1:T(4,128)S(1)}, s32[2]{0:T(128)S(1)}, s32[2,32,2]{1,2,0:T(2,128)S(1)}, s32[]{:T(128)}, /*index=5*/bf16[2,32,128...) while((s32[]{:T(128)}, f32[4,128,256]{2,0,1:T(4,128)S(1)}, ...), condition=%wide.region_1.3_spmd.clone, body=%wide.region_0.2_spmd.clone.sunk | while | flops 278136320 | bytes 12588737 | solution.py:60
  19.6 0.6 dynamic_slice.45
  22.2 2.0 gather_fusion
  24.2 2.7 %fusion.70 = bf16[32,128,256]{2,1,0:T(8,128)(2,1)S(1)} fusion(bf16[32,128,256]{2,1,0:T(8,128)(2,1)} %gather_fusion, pred[32]{0:T(512)(128)(4,1)S(1)} %get-tuple-element.273, bf16[2,32,128,128]{3,2,1,0:T(8,128)(2,1)} %get-tuple-element.310, s32[]{:T(128)S(6)} %select_n.94), kind=kOutput, calls=%fused_computation.6.clone.1 | convolution fusion | flops 269484032 | bytes 5242916 | tf_op jit(solution)/shard_map/while/body/eval_jaxpr/sij,sjf->sif/dot_general | solution.py:43
  27.6 0.7 add_compare_fusion.4
  28.2 1.4 fusion.71
  29.7 0.6 dynamic_slice.45
  32.3 2.0 gather_fusion
  34.3 2.7 %fusion.70 = bf16[32,128,256]{2,1,0:T(8,128)(2,1)S(1)} fusion(bf16[32,128,256]{2,1,0:T(8,128)(2,1)} %gather_fusion, pred[32]{0:T(512)(128)(4,1)S(1)} %get-tuple-element.273, bf16[2,32,128,128]{3,2,1,0:T(8,128)(2,1)} %get-tuple-element.310, s32[]{:T(128)S(6)} %select_n.94), kind=kOutput, calls=%fused_computation.6.clone.1 | convolution fusion | flops 269484032 | bytes 5242916 | tf_op jit(solution)/shard_map/while/body/eval_jaxpr/sij,sjf->sif/dot_general | solution.py:43
  37.6 0.7 add_compare_fusion.4
  38.3 1.4 fusion.71
  39.7 0.9 copy.10
  40.6 0.0 reduce-scatter.3.cloned.1.call-update
  40.7 0.0 all-reduce.2.cloned.1.call-start
  40.7 22.0 %reduce-scatter.3.cloned.1.call-done = f32[128,256]{1,0:T(8,128)} async-done(((f32[512,256]{1,0:T(8,128)}), f32[128,256]{1,0:T(8,128)}) %reduce-scatter.3.cloned.1.call-update) | async-done | bytes 131088 | tf_op jit(solution)/shard_map/reduce_scatter | solution.py:66
  62.7 0.9 convert_element_type.15
  63.7 1.3 collective-permute-start
  65.0 0.0 copy-done.2
  65.0 0.0 copy-done.3
  65.0 0.2 fusion.44
  65.2 1.6 collective-permute-done
  66.8 0.2 convolution_convert_fusion
  67.0 8.9 %all_gather.7 = bf16[512,256]{1,0:T(8,128)(2,1)S(1)} all-gather(bf16[128,256]{1,0:T(8,128)(2,1)S(1)} %convolution_convert_fusion), channel_id=1, replica_groups=mesh['section'=2,'row'=4,'col'=4] {'row'}, dimensions={0}, use_global_device_ids=true | all-gather | bytes 327680 | tf_op jit(solution)/shard_map/all_gather | solution.py:35
  75.9 0.9 fusion.40
  76.9 0.0 all-reduce.2.cloned.1.call-update
  76.9 0.0 reduce-scatter.5.cloned.1.call-start
  77.0 19.5 %while.23 = (s32[]{:T(128)}, f32[4,128,256]{2,0,1:T(4,128)S(1)}, s32[2]{0:T(128)S(1)}, s32[2,32,2]{1,2,0:T(2,128)S(1)}, s32[]{:T(128)}, /*index=5*/bf16[2,32,128...) while((s32[]{:T(128)}, f32[4,128,256]{2,0,1:T(4,128)S(1)}, ...), condition=%wide.region_5.7_spmd.clone, body=%wide.region_4.6_spmd.clone.sunk | while | flops 278136320 | bytes 12588737 | solution.py:60
  77.0 0.6 dynamic_slice.48
  79.3 2.0 gather_fusion.1
  81.3 2.7 %fusion.76 = bf16[32,128,256]{2,1,0:T(8,128)(2,1)S(1)} fusion(bf16[32,128,256]{2,1,0:T(8,128)(2,1)} %gather_fusion.1, pred[32]{0:T(512)(128)(4,1)S(1)} %get-tuple-element.282, bf16[2,32,128,128]{3,2,1,0:T(8,128)(2,1)} %get-tuple-element.343, s32[]{:T(128)S(6)} %select_n.96), kind=kOutput, calls=%fused_computation.28.clone.1 | convolution fusion | flops 269484032 | bytes 5242916 | tf_op jit(solution)/shard_map/while/body/eval_jaxpr/sij,sjf->sif/dot_general | solution.py:43
  84.6 0.7 add_compare_fusion.5
  85.2 1.4 fusion.77
  86.7 0.6 dynamic_slice.48
  89.0 2.0 gather_fusion.1
  91.0 2.7 %fusion.76 = bf16[32,128,256]{2,1,0:T(8,128)(2,1)S(1)} fusion(bf16[32,128,256]{2,1,0:T(8,128)(2,1)} %gather_fusion.1, pred[32]{0:T(512)(128)(4,1)S(1)} %get-tuple-element.282, bf16[2,32,128,128]{3,2,1,0:T(8,128)(2,1)} %get-tuple-element.343, s32[]{:T(128)S(6)} %select_n.96), kind=kOutput, calls=%fused_computation.28.clone.1 | convolution fusion | flops 269484032 | bytes 5242916 | tf_op jit(solution)/shard_map/while/body/eval_jaxpr/sij,sjf->sif/dot_general | solution.py:43
  94.3 0.7 add_compare_fusion.5
  95.0 1.4 fusion.77
  96.4 0.0 copy-start.1
  96.4 0.9 copy.12
  97.3 0.0 reduce-scatter.5.cloned.1.call-update
  97.3 83.9 %all-reduce.2.cloned.1.call-done = f32[256,256]{0,1:T(8,128)} async-done(((f32[256,256]{0,1:T(8,128)}), f32[256,256]{0,1:T(8,128)}) %all-reduce.2.cloned.1.call-update) | async-done | bytes 262160 | tf_op jit(solution)/shard_map/psum | solution.py:91
  181.2 1.0 multiply_bitcast_fusion
  182.2 0.8 copy.13
  183.0 21.3 %reduce-scatter.5.cloned.1.call-done = f32[128,256]{1,0:T(8,128)} async-done(((f32[512,256]{1,0:T(8,128)}), f32[128,256]{1,0:T(8,128)}) %reduce-scatter.5.cloned.1.call-update) | async-done | bytes 131088 | tf_op jit(solution)/shard_map/reduce_scatter | solution.py:66
  204.3 0.0 copy-done.1
  204.3 1.5 select_bitcast_fusion
  (21 shorter events, 0.1 us)
Async XLA Ops:
  7.2 0.9 copy-start
  7.2 55.6 %reduce-scatter.3.cloned.1.call-start = ((), (), s32[]{:S(2)}) async-start(), calls=%async_computation.2 | async-start | bytes 655360 | tf_op jit(solution)/shard_map/reduce_scatter | solution.py:66
  19.6 45.4 %copy-start.2 = (bf16[1,128,256]{2,1,0:T(8,128)(2,1)S(1)}, bf16[1,128,256]{2,1,0:T(8,128)(2,1)}, u32[]{:S(2)}) copy-start(bf16[1,128,256]{2,1,0:T(8,128)(2,1)} %param.15) | copy-start | bytes 196612
  19.6 45.4 %copy-start.3 = (bf16[128,256]{1,0:T(8,128)(2,1)S(1)}, bf16[128,256]{1,0:T(8,128)(2,1)}, u32[]{:S(2)}) copy-start(bf16[128,256]{1,0:T(8,128)(2,1)} %param.13) | copy-start | bytes 196612
  40.7 140.5 %all-reduce.2.cloned.1.call-start = ((), (), s32[]{:S(2)}) async-start(), calls=%async_computation.3 | async-start | bytes 524288 | tf_op jit(solution)/shard_map/psum | solution.py:91
  63.7 3.1 %collective-permute-start = (bf16[128,256]{1,0:T(8,128)(2,1)S(1)}, bf16[128,256]{1,0:T(8,128)(2,1)S(1)}, u32[]{:S(2)}, u32[]{:S(2)}) collective-permute-start(bf16[128,256]{1,0:T(8,128)(2,1)S(1)} %convert_element_type.15), channel_id=1, source_target_pairs={{16,0},{17,1},{18,2},{19,3},{20,4},{21,5},{22,6},{23,7},{24,8},{25... | collective-permute-start | bytes 196616 | tf_op jit(solution)/shard_map/ppermute | solution.py:11
  76.9 127.4 %reduce-scatter.5.cloned.1.call-start = ((), (), s32[]{:S(2)}) async-start(), calls=%async_computation.4 | async-start | bytes 655360 | tf_op jit(solution)/shard_map/reduce_scatter | solution.py:66
  96.4 107.9 %copy-start.1 = (f32[128,256]{1,0:T(8,128)S(1)}, f32[128,256]{1,0:T(8,128)}, u32[]{:S(2)}) copy-start(f32[128,256]{1,0:T(8,128)} %reduce-scatter.3.cloned.1.call-done) | copy-start | bytes 393220
Sparse Core Ops, SparseCore 0:
  40.8 21.9 reduce-scatter.2
  77.0 104.1 all-reduce.1
  183.6 20.6 reduce-scatter.4
where the time goes:
time: 213 us; the launch traced here: 212 us
  waiting for transfers between devices  129 us (61%)
  blocking collectives  19.4 us (9%)
  matrix products  18.1 us (8%)
  local copies, waits for them, and re-layouts  13.9 us (7%)
  between operations  13.9 us (7%)
  loops' own time  9.92 us (5%)
  other arithmetic  6.98 us (3%)
    psum x1, waiting for transfers between devices, on_device(): total_weight = lax.psum(local_weight, ('row', 'col'))  83.9 us
    reduce_scatter x2, waiting for transfers between devices, reduce_col(): lax.psum_scatter(block_total(source, col_blocks), 'col', scatter_dimensio...  43.3 us
    all_gather x2, blocking collectives, spread(): return lax.all_gather(row_grad, 'row', axis=0, tiled=True)  19.4 us
    dot_general x4, matrix products, group_term(): jnp.einsum('sij,sjf->sif', blocks_here, picked, preferred_element_type=jn...  10.8 us
    another operation x2, loops' own time, block_total(): lax.scan(scan_step, start_total, jnp.arange(groups, dtype=jnp.int32))  9.92 us
    gather x4, local copies, waits for them, and re-layouts, group_term(): picked = jnp.take(col_blocks, slots_here[:, 1], axis=0)  8.08 us
    dot_general x4, matrix products, group_term(): return total + jnp.einsum('bs,sif->bif', select, products)  5.75 us
  transfers between devices with their start and end apart: 4, of which 4 were waited for; matrix products, arithmetic and copies ran while one was open for 8% of the time, Pallas kernels for 0%

commit v1 on v0

--- a/solution.py
+++ b/solution.py
@@ -88,7 +88,7 @@
     second_weight, second_grad = backward_step(received)
     local_weight = jnp.where(upper, first_weight, second_weight)
     feature_block = jnp.where(upper, first_grad, second_grad)
-    total_weight = lax.psum(local_weight, ("row", "col"))
+    total_weight = lax.psum(lax.psum(local_weight, "col"), "row")
     node_total = node_rows * lax.axis_size("row") * lax.axis_size("col")
     weight_grad = (total_weight * (1.0 / math.sqrt(node_total)))[None]
     return (weight_grad, feature_block[None])

time: 213 us -> 180 us (0.85)
  waiting for transfers between devices: 129 us -> 95 us
    psum x1 -> x2, waiting for transfers between devices: 83.9 us -> 49.4 us  [on_device(): total_weight = lax.psum(lax.psum(local_weight, 'col'), 'row')]
  transfers between devices with their start and end apart: 4 -> 5, of which waited for: 4 -> 5; matrix products, arithmetic and copies ran while one was open for 8% -> 10% of each run, Pallas kernels for 0% -> 0%
where the time goes in v1:
time: 180 us; the launch traced here: 179 us
  waiting for transfers between devices  95 us (53%)
  blocking collectives  19.4 us (11%)
  matrix products  18 us (10%)
  local copies, waits for them, and re-layouts  13.9 us (8%)
  between operations  13.9 us (8%)
  loops' own time  10.6 us (6%)
  other arithmetic  6.98 us (4%)
    psum x2, waiting for transfers between devices, on_device(): total_weight = lax.psum(lax.psum(local_weight, 'col'), 'row')  49.4 us
    reduce_scatter x2, waiting for transfers between devices, reduce_col(): lax.psum_scatter(block_total(source, col_blocks), 'col', scatter_dimensio...  44 us
    all_gather x2, blocking collectives, spread(): return lax.all_gather(row_grad, 'row', axis=0, tiled=True)  19.4 us
    dot_general x4, matrix products, group_term(): jnp.einsum('sij,sjf->sif', blocks_here, picked, preferred_element_type=jn...  10.8 us
    another operation x2, loops' own time, block_total(): lax.scan(scan_step, start_total, jnp.arange(groups, dtype=jnp.int32))  10.6 us
    gather x4, local copies, waits for them, and re-layouts, group_term(): picked = jnp.take(col_blocks, slots_here[:, 1], axis=0)  8.08 us
    dot_general x4, matrix products, group_term(): return total + jnp.einsum('bs,sif->bif', select, products)  5.75 us
  transfers between devices with their start and end apart: 5, of which 5 were waited for; matrix products, arithmetic and copies ran while one was open for 10% of the time, Pallas kernels for 0%

profile of v1, /device:TPU:0, one launch (start us, length us, event | category | flops | bytes accessed | tf_op | source)
XLA Modules:
  0.0 179.3 jit_solution(14495105843355704719)
XLA Ops:
  7.2 0.0 copy-start
  7.2 0.0 reduce-scatter.3.cloned.1.call-start
  7.2 0.9 broadcast_compare_fusion
  8.1 0.0 copy-done
  8.1 0.2 convolution_convert_fusion.1
  8.3 10.5 %all_gather.6 = bf16[512,256]{1,0:T(8,128)(2,1)S(1)} all-gather(bf16[128,256]{1,0:T(8,128)(2,1)S(1)} %convolution_convert_fusion.1), channel_id=1, replica_groups=mesh['section'=2,'row'=4,'col'=4] {'row'}, dimensions={0}, use_global_device_ids=true | all-gather | bytes 327680 | tf_op jit(solution)/shard_map/all_gather | solution.py:35
  18.8 0.8 reshape_squeeze.7
  19.6 0.0 copy-start.2
  19.6 0.0 copy-start.3
  19.6 20.1 %while.22 = (s32[]{:T(128)}, f32[4,128,256]{2,0,1:T(4,128)S(1)}, s32[2]{0:T(128)S(1)}, s32[2,32,2]{1,2,0:T(2,128)S(1)}, s32[]{:T(128)}, /*index=5*/bf16[2,32,128...) while((s32[]{:T(128)}, f32[4,128,256]{2,0,1:T(4,128)S(1)}, ...), condition=%wide.region_1.3_spmd.clone, body=%wide.region_0.2_spmd.clone.sunk | while | flops 278136320 | bytes 12588737 | solution.py:60
  19.6 0.6 dynamic_slice.45
  22.2 2.0 %gather_fusion = bf16[32,128,256]{2,1,0:T(8,128)(2,1)} fusion(bf16[4,128,256]{2,1,0:T(8,128)(2,1)S(1)} %get-tuple-element.311, s32[1024]{0:T(1024)S(1)} %pad_clamp_fusion.4), kind=kCustom, calls=%fused_computation.clone.clone.1 | custom fusion | bytes 4194432 | tf_op jit(solution)/shard_map/while/body/eval_jaxpr/jit(_take)/gather | solution.py:42
  24.2 2.7 %fusion.70 = bf16[32,128,256]{2,1,0:T(8,128)(2,1)S(1)} fusion(bf16[32,128,256]{2,1,0:T(8,128)(2,1)} %gather_fusion, pred[32]{0:T(512)(128)(4,1)S(1)} %get-tuple-element.273, bf16[2,32,128,128]{3,2,1,0:T(8,128)(2,1)} %get-tuple-element.310, s32[]{:T(128)S(6)} %select_n.94), kind=kOutput, calls=%fused_computation.6.clone.1 | convolution fusion | flops 269484032 | bytes 5242916 | tf_op jit(solution)/shard_map/while/body/eval_jaxpr/sij,sjf->sif/dot_general | solution.py:43
  27.6 0.7 add_compare_fusion.4
  28.2 1.4 fusion.71
  29.7 0.6 dynamic_slice.45
  32.3 2.0 %gather_fusion = bf16[32,128,256]{2,1,0:T(8,128)(2,1)} fusion(bf16[4,128,256]{2,1,0:T(8,128)(2,1)S(1)} %get-tuple-element.311, s32[1024]{0:T(1024)S(1)} %pad_clamp_fusion.4), kind=kCustom, calls=%fused_computation.clone.clone.1 | custom fusion | bytes 4194432 | tf_op jit(solution)/shard_map/while/body/eval_jaxpr/jit(_take)/gather | solution.py:42
  34.3 2.7 %fusion.70 = bf16[32,128,256]{2,1,0:T(8,128)(2,1)S(1)} fusion(bf16[32,128,256]{2,1,0:T(8,128)(2,1)} %gather_fusion, pred[32]{0:T(512)(128)(4,1)S(1)} %get-tuple-element.273, bf16[2,32,128,128]{3,2,1,0:T(8,128)(2,1)} %get-tuple-element.310, s32[]{:T(128)S(6)} %select_n.94), kind=kOutput, calls=%fused_computation.6.clone.1 | convolution fusion | flops 269484032 | bytes 5242916 | tf_op jit(solution)/shard_map/while/body/eval_jaxpr/sij,sjf->sif/dot_general | solution.py:43
  37.6 0.7 add_compare_fusion.4
  38.3 1.4 fusion.71
  39.7 0.9 copy.10
  40.6 0.0 reduce-scatter.3.cloned.1.call-update
  40.7 0.0 all-reduce.3.cloned.1.call-start
  40.7 22.0 %reduce-scatter.3.cloned.1.call-done = f32[128,256]{1,0:T(8,128)} async-done(((f32[512,256]{1,0:T(8,128)}), f32[128,256]{1,0:T(8,128)}) %reduce-scatter.3.cloned.1.call-update) | async-done | bytes 131088 | tf_op jit(solution)/shard_map/reduce_scatter | solution.py:66
  62.7 0.9 convert_element_type.15
  63.7 1.3 collective-permute-start
  65.0 0.0 copy-done.2
  65.0 0.0 copy-done.3
  65.0 0.2 fusion.44
  65.2 1.6 collective-permute-done
  66.8 0.9 fusion.40
  67.7 0.0 all-reduce.3.cloned.1.call-update
  67.7 0.0 all-reduce.5.cloned.1.call-start
  67.8 0.2 convolution_convert_fusion
  68.0 8.9 %all_gather.7 = bf16[512,256]{1,0:T(8,128)(2,1)S(1)} all-gather(bf16[128,256]{1,0:T(8,128)(2,1)S(1)} %convolution_convert_fusion), channel_id=1, replica_groups=mesh['section'=2,'row'=4,'col'=4] {'row'}, dimensions={0}, use_global_device_ids=true | all-gather | bytes 327680 | tf_op jit(solution)/shard_map/all_gather | solution.py:35
  76.9 24.6 %all-reduce.3.cloned.1.call-done = f32[256,256]{0,1:T(8,128)} async-done(((f32[256,256]{0,1:T(8,128)}), f32[256,256]{0,1:T(8,128)}) %all-reduce.3.cloned.1.call-update) | async-done | bytes 262160 | tf_op jit(solution)/shard_map/psum | solution.py:91
  101.5 0.0 all-reduce.5.cloned.1.call-update
  101.6 0.0 reduce-scatter.5.cloned.1.call-start
  101.6 20.1 %while.23 = (s32[]{:T(128)}, f32[4,128,256]{2,0,1:T(4,128)S(1)}, s32[2]{0:T(128)S(1)}, s32[2,32,2]{1,2,0:T(2,128)S(1)}, s32[]{:T(128)}, /*index=5*/bf16[2,32,128...) while((s32[]{:T(128)}, f32[4,128,256]{2,0,1:T(4,128)S(1)}, ...), condition=%wide.region_6.8_spmd.clone, body=%wide.region_5.7_spmd.clone.sunk | while | flops 278136320 | bytes 12588737 | solution.py:60
  101.6 0.6 dynamic_slice.48
  104.2 2.0 %gather_fusion.1 = bf16[32,128,256]{2,1,0:T(8,128)(2,1)} fusion(bf16[4,128,256]{2,1,0:T(8,128)(2,1)S(1)} %get-tuple-element.344, s32[1024]{0:T(1024)S(1)} %pad_clamp_fusion.5), kind=kCustom, calls=%fused_computation.1.clone.clone.1 | custom fusion | bytes 4194432 | tf_op jit(solution)/shard_map/while/body/eval_jaxpr/jit(_take)/gather | solution.py:42
  106.2 2.7 %fusion.76 = bf16[32,128,256]{2,1,0:T(8,128)(2,1)S(1)} fusion(bf16[32,128,256]{2,1,0:T(8,128)(2,1)} %gather_fusion.1, pred[32]{0:T(512)(128)(4,1)S(1)} %get-tuple-element.282, bf16[2,32,128,128]{3,2,1,0:T(8,128)(2,1)} %get-tuple-element.343, s32[]{:T(128)S(6)} %select_n.96), kind=kOutput, calls=%fused_computation.28.clone.1 | convolution fusion | flops 269484032 | bytes 5242916 | tf_op jit(solution)/shard_map/while/body/eval_jaxpr/sij,sjf->sif/dot_general | solution.py:43
  109.6 0.7 add_compare_fusion.5
  110.3 1.4 fusion.77
  111.7 0.6 dynamic_slice.48
  114.3 2.0 %gather_fusion.1 = bf16[32,128,256]{2,1,0:T(8,128)(2,1)} fusion(bf16[4,128,256]{2,1,0:T(8,128)(2,1)S(1)} %get-tuple-element.344, s32[1024]{0:T(1024)S(1)} %pad_clamp_fusion.5), kind=kCustom, calls=%fused_computation.1.clone.clone.1 | custom fusion | bytes 4194432 | tf_op jit(solution)/shard_map/while/body/eval_jaxpr/jit(_take)/gather | solution.py:42
  116.3 2.7 %fusion.76 = bf16[32,128,256]{2,1,0:T(8,128)(2,1)S(1)} fusion(bf16[32,128,256]{2,1,0:T(8,128)(2,1)} %gather_fusion.1, pred[32]{0:T(512)(128)(4,1)S(1)} %get-tuple-element.282, bf16[2,32,128,128]{3,2,1,0:T(8,128)(2,1)} %get-tuple-element.343, s32[]{:T(128)S(6)} %select_n.96), kind=kOutput, calls=%fused_computation.28.clone.1 | convolution fusion | flops 269484032 | bytes 5242916 | tf_op jit(solution)/shard_map/while/body/eval_jaxpr/sij,sjf->sif/dot_general | solution.py:43
  119.7 0.7 add_compare_fusion.5
  120.3 1.4 fusion.77
  121.8 0.0 copy-start.1
  121.8 0.9 copy.12
  122.7 0.0 reduce-scatter.5.cloned.1.call-update
  122.7 24.8 %all-reduce.5.cloned.1.call-done = f32[256,256]{0,1:T(8,128)} async-done(((f32[256,256]{0,1:T(8,128)}), f32[256,256]{0,1:T(8,128)}) %all-reduce.5.cloned.1.call-update) | async-done | bytes 262160 | tf_op jit(solution)/shard_map/psum | solution.py:91
  147.5 1.0 multiply_bitcast_fusion
  148.4 0.8 copy.13
  149.3 22.0 %reduce-scatter.5.cloned.1.call-done = f32[128,256]{1,0:T(8,128)} async-done(((f32[512,256]{1,0:T(8,128)}), f32[128,256]{1,0:T(8,128)}) %reduce-scatter.5.cloned.1.call-update) | async-done | bytes 131088 | tf_op jit(solution)/shard_map/reduce_scatter | solution.py:66
  171.2 0.0 copy-done.1
  171.2 1.5 select_bitcast_fusion
  (21 shorter events, 0.1 us)
Async XLA Ops:
  7.2 0.9 copy-start
  7.2 55.6 %reduce-scatter.3.cloned.1.call-start = ((), (), s32[]{:S(2)}) async-start(), calls=%async_computation.2 | async-start | bytes 655360 | tf_op jit(solution)/shard_map/reduce_scatter | solution.py:66
  19.6 45.4 %copy-start.2 = (bf16[1,128,256]{2,1,0:T(8,128)(2,1)S(1)}, bf16[1,128,256]{2,1,0:T(8,128)(2,1)}, u32[]{:S(2)}) copy-start(bf16[1,128,256]{2,1,0:T(8,128)(2,1)} %param.15) | copy-start | bytes 196612
  19.6 45.4 %copy-start.3 = (bf16[128,256]{1,0:T(8,128)(2,1)S(1)}, bf16[128,256]{1,0:T(8,128)(2,1)}, u32[]{:S(2)}) copy-start(bf16[128,256]{1,0:T(8,128)(2,1)} %param.13) | copy-start | bytes 196612
  40.7 60.9 %all-reduce.3.cloned.1.call-start = ((), (), s32[]{:S(2)}) async-start(), calls=%async_computation.3 | async-start | bytes 524288 | tf_op jit(solution)/shard_map/psum | solution.py:91
  63.7 3.1 %collective-permute-start = (bf16[128,256]{1,0:T(8,128)(2,1)S(1)}, bf16[128,256]{1,0:T(8,128)(2,1)S(1)}, u32[]{:S(2)}, u32[]{:S(2)}) collective-permute-start(bf16[128,256]{1,0:T(8,128)(2,1)S(1)} %convert_element_type.15), channel_id=1, source_target_pairs={{16,0},{17,1},{18,2},{19,3},{20,4},{21,5},{22,6},{23,7},{24,8},{25... | collective-permute-start | bytes 196616 | tf_op jit(solution)/shard_map/ppermute | solution.py:11
  67.7 79.7 %all-reduce.5.cloned.1.call-start = ((), (), s32[]{:S(2)}) async-start(), calls=%async_computation.4 | async-start | bytes 524288 | tf_op jit(solution)/shard_map/psum | solution.py:91
  101.6 69.7 %reduce-scatter.5.cloned.1.call-start = ((), (), s32[]{:S(2)}) async-start(), calls=%async_computation.5 | async-start | bytes 655360 | tf_op jit(solution)/shard_map/reduce_scatter | solution.py:66
  121.8 49.5 %copy-start.1 = (f32[128,256]{1,0:T(8,128)S(1)}, f32[128,256]{1,0:T(8,128)}, u32[]{:S(2)}) copy-start(f32[128,256]{1,0:T(8,128)} %reduce-scatter.3.cloned.1.call-done) | copy-start | bytes 393220
Sparse Core Ops, SparseCore 0:
  40.8 21.9 reduce-scatter.2
  67.9 33.6 all-reduce.2
  104.7 42.6 all-reduce.4
  149.6 21.6 reduce-scatter.4
